TPU v7x, 32 devices: a whole 2x2x4 slice. The times are simulated.
32 devices in a mesh: row: 16 (over z, y, x), col: 2 (over core).
Axes of the slice: x: 2, y: 2, z: 4, core: 2. Of those that a mesh axis runs over, the one named last changes fastest.
Arguments:
- samples: bfloat16 [32768, 8192], P('row', 'col'), may hold values from -0.046875 to 0.046875
- targets: float32 [32768, 128], P('row'), may hold values from -6 to 6
- factor_inv: float32 [2, 4096, 4096], P('col', None, 'row'), may hold values from -1 to 1, as said below
Outputs:
- solution: float32 [8192, 128], P('col')
- residual: float32 [32768, 128], P('row')
Inputs may be any that keep to these rules, and one draw needn't show every extreme that they name: Each factor_inv[j] is lower triangular with a positive diagonal.
All inputs are finite; a program needn't handle non-finite values.
Results may differ from a plain program's by a relative error of at most 0.0039.
Values sent between devices are 32-bit elements; how exact they have to be, the bound alone decides.
A program may use at most 128 MiB of HBM per device.

v0:
```python
import jax
import jax.numpy as jnp
from jax import lax
from jax.sharding import PartitionSpec as P

ROUNDS = 3
ridge_weight = 0.5


def run_group(samples, residual, inverse, own_rows, offset, relaxation):
    solution = jnp.zeros((samples.shape[1], residual.shape[1]), jnp.float32)
    for sweep in range(ROUNDS):
        res16 = residual.astype(jnp.bfloat16)
        part_grad = jnp.einsum("rb,rk->bk", samples, res16, preferred_element_type=jnp.float32)
        own_solution = lax.dynamic_slice_in_dim(solution, offset, own_rows, 0)
        grad_total = lax.psum(part_grad, "row")
        grad_own = (
            lax.dynamic_slice_in_dim(grad_total, offset, own_rows, 0) - ridge_weight * own_solution
        )
        term = jnp.dot(inverse, grad_own, precision=lax.Precision.HIGHEST)
        image = lax.psum(term, "row")
        update_own = jnp.einsum("bc,bk->ck", inverse, image, precision=lax.Precision.HIGHEST)
        update = lax.all_gather(update_own, "row", axis=0, tiled=True)
        solution = solution + relaxation * update
        change = jnp.dot(samples, update.astype(jnp.bfloat16), preferred_element_type=jnp.float32)
        residual = residual - relaxation * lax.psum(change, "col")
    return (solution, residual)


def per_device(samples, targets, factor_inv):
    inverse = factor_inv[0]
    own_rows = inverse.shape[1]
    offset = lax.axis_index("row") * own_rows
    relaxation = 1.0 / lax.axis_size("col")
    solution, residual = run_group(samples, targets, inverse, own_rows, offset, relaxation)
    return (solution, residual)


def solution(mesh):
    in_specs = (P("row", "col"), P("row", None), P("col", None, "row"))
    out_specs = (P("col", None), P("row", None))
    return jax.shard_map(
        per_device, mesh=mesh, in_specs=in_specs, out_specs=out_specs, check_vma=False
    )
```

profile of v0, /device:TPU:0, one launch (start us, length us, event | category | flops | bytes accessed | tf_op | source)
XLA Modules:
  0.0 1128.9 jit_solution(2055085821760850830)
XLA Ops:
  7.2 11.9 %fusion.23 = f32[4096,128]{1,0:T(8,128)} fusion(bf16[2048,4096]{1,0:T(8,128)(2,1)} %param.3, f32[2048,128]{1,0:T(8,128)} %param.4), kind=kOutput, calls=%fused_computation.31 | convolution fusion | flops 2147745792 | bytes 19922944 | tf_op jit(solution)/shard_map/rb,rk->bk/dot_general | solution.py:14
  19.2 128.8 %all-reduce.10.cloned.1.call-done = f32[4096,128]{1,0:T(8,128)} async-done(((f32[4096,128]{1,0:T(8,128)}), f32[4096,128]{1,0:T(8,128)}) %all-reduce.10.cloned.1.call-update) | async-done | bytes 2097168 | tf_op jit(solution)/shard_map/psum | solution.py:16
  148.0 8.1 convolution_bitcast_fusion.4
  156.1 125.4 %all-reduce.12.cloned.1.call-done = f32[4096,128]{0,1:T(8,128)} async-done(((f32[4096,128]{0,1:T(8,128)}), f32[4096,128]{0,1:T(8,128)}) %all-reduce.12.cloned.1.call-update) | async-done | bytes 2097168 | tf_op jit(solution)/shard_map/psum | solution.py:21
  281.6 5.6 fusion.9
  287.7 60.7 %all-gather.4.cloned.1.call-done = f32[4096,128]{0,1:T(8,128)} async-done(((f32[256,128]{0,1:T(8,128)}), f32[4096,128]{0,1:T(8,128)}) %all-gather.4.cloned.1.call-update) | async-done | bytes 2097168 | tf_op jit(solution)/shard_map/all_gather | solution.py:23
  348.4 13.0 %convolution_bitcast_fusion.7 = f32[2048,128]{0,1:T(8,128)} fusion(bf16[2048,4096]{1,0:T(8,128)(2,1)} %param.3, f32[4096,128]{0,1:T(8,128)} %all-gather.4.cloned.1.call-done), kind=kOutput, calls=%fused_computation.16 | convolution fusion | flops 2148007936 | bytes 19922944 | tf_op jit(solution)/shard_map/dot_general | solution.py:25
  361.9 17.5 %all-reduce.14.cloned.1.call-done = f32[2048,128]{0,1:T(8,128)} async-done(((f32[2048,128]{0,1:T(8,128)}), f32[2048,128]{0,1:T(8,128)}) %all-reduce.14.cloned.1.call-update) | async-done | bytes 1048592 | tf_op jit(solution)/shard_map/psum | solution.py:26
  379.4 9.8 convolution_bitcast_fusion.1
  392.3 124.2 %all-reduce.16.cloned.1.call-done = f32[4096,128]{0,1:T(8,128)} async-done(((f32[4096,128]{0,1:T(8,128)}), f32[4096,128]{0,1:T(8,128)}) %all-reduce.16.cloned.1.call-update) | async-done | bytes 2097168 | tf_op jit(solution)/shard_map/psum | solution.py:16
  516.5 8.0 convolution_bitcast_fusion.3
  524.7 125.2 %all-reduce.18.cloned.1.call-done = f32[4096,128]{0,1:T(8,128)} async-done(((f32[4096,128]{0,1:T(8,128)}), f32[4096,128]{0,1:T(8,128)}) %all-reduce.18.cloned.1.call-update) | async-done | bytes 2097168 | tf_op jit(solution)/shard_map/psum | solution.py:21
  649.9 5.6 fusion.12
  655.6 61.2 %all-gather.6.cloned.1.call-done = f32[4096,128]{0,1:T(8,128)} async-done(((f32[256,128]{0,1:T(8,128)}), f32[4096,128]{0,1:T(8,128)}) %all-gather.6.cloned.1.call-update) | async-done | bytes 2097168 | tf_op jit(solution)/shard_map/all_gather | solution.py:23
  716.8 13.0 %convolution_bitcast_fusion.6 = f32[2048,128]{0,1:T(8,128)} fusion(bf16[2048,4096]{1,0:T(8,128)(2,1)} %param.3, f32[4096,128]{0,1:T(8,128)} %all-gather.6.cloned.1.call-done), kind=kOutput, calls=%fused_computation.15 | convolution fusion | flops 2148007936 | bytes 19922944 | tf_op jit(solution)/shard_map/dot_general | solution.py:25
  729.9 17.9 %all-reduce.20.cloned.1.call-done = f32[2048,128]{0,1:T(8,128)} async-done(((f32[2048,128]{0,1:T(8,128)}), f32[2048,128]{0,1:T(8,128)}) %all-reduce.20.cloned.1.call-update) | async-done | bytes 1048592 | tf_op jit(solution)/shard_map/psum | solution.py:26
  747.8 10.2 convolution_bitcast_fusion
  761.4 123.8 %all-reduce.22.cloned.1.call-done = f32[4096,128]{0,1:T(8,128)} async-done(((f32[4096,128]{0,1:T(8,128)}), f32[4096,128]{0,1:T(8,128)}) %all-reduce.22.cloned.1.call-update) | async-done | bytes 2097168 | tf_op jit(solution)/shard_map/psum | solution.py:16
  885.3 7.9 convolution_bitcast_fusion.2
  893.3 125.4 %all-reduce.24.cloned.1.call-done = f32[4096,128]{0,1:T(8,128)} async-done(((f32[4096,128]{0,1:T(8,128)}), f32[4096,128]{0,1:T(8,128)}) %all-reduce.24.cloned.1.call-update) | async-done | bytes 2097168 | tf_op jit(solution)/shard_map/psum | solution.py:21
  1018.7 5.6 fusion.15
  1024.4 61.2 %all-gather.8.cloned.1.call-done = f32[4096,128]{0,1:T(8,128)} async-done(((f32[256,128]{0,1:T(8,128)}), f32[4096,128]{0,1:T(8,128)}) %all-gather.8.cloned.1.call-update) | async-done | bytes 2097168 | tf_op jit(solution)/shard_map/all_gather | solution.py:23
  1085.6 13.2 %convolution_bitcast_fusion.5 = f32[2048,128]{0,1:T(8,128)} fusion(bf16[2048,4096]{1,0:T(8,128)(2,1)} %param.3, f32[4096,128]{0,1:T(8,128)} %all-gather.8.cloned.1.call-done), kind=kOutput, calls=%fused_computation.14 | convolution fusion | flops 2148007936 | bytes 19922944 | tf_op jit(solution)/shard_map/dot_general | solution.py:25
  1105.3 11.5 %all-reduce.26.cloned.1.call-done = f32[2048,128]{0,1:T(8,128)} async-done(((f32[2048,128]{0,1:T(8,128)}), f32[2048,128]{0,1:T(8,128)}) %all-reduce.26.cloned.1.call-update) | async-done | bytes 1048592 | tf_op jit(solution)/shard_map/psum | solution.py:26
  (41 shorter events, 19.5 us)
Async XLA Ops:
  7.2 140.8 %all-reduce.10.cloned.1.call-start = ((), (), s32[]{:S(2)}) async-start(), calls=%async_computation | async-start | bytes 4194304 | tf_op jit(solution)/shard_map/psum | solution.py:16
  19.1 262.4 %all-reduce.12.cloned.1.call-start = ((), (), s32[]{:S(2)}) async-start(), calls=%async_computation.1 | async-start | bytes 4194304 | tf_op jit(solution)/shard_map/psum | solution.py:21
  156.1 192.4 %all-gather.4.cloned.1.call-start = ((), (), s32[]{:S(2)}) async-start(), calls=%async_computation.2 | async-start | bytes 2228224 | tf_op jit(solution)/shard_map/all_gather | solution.py:23
  287.2 74.4 %copy-start.4 = (f32[2048,128]{1,0:T(8,128)S(1)}, f32[2048,128]{1,0:T(8,128)}, u32[]{:S(2)}) copy-start(f32[2048,128]{1,0:T(8,128)} %param.4) | copy-start | bytes 3145732
  287.2 92.2 %all-reduce.14.cloned.1.call-start = ((), (), s32[]{:S(2)}) async-start(), calls=%async_computation.3 | async-start | bytes 2097152 | tf_op jit(solution)/shard_map/psum | solution.py:26
  361.5 155.1 %all-reduce.16.cloned.1.call-start = ((), (), s32[]{:S(2)}) async-start(), calls=%async_computation.4 | async-start | bytes 4194304 | tf_op jit(solution)/shard_map/psum | solution.py:16
  389.2 1.6 copy-start
  389.2 260.7 %all-reduce.18.cloned.1.call-start = ((), (), s32[]{:S(2)}) async-start(), calls=%async_computation.5 | async-start | bytes 4194304 | tf_op jit(solution)/shard_map/psum | solution.py:21
  524.5 192.3 %all-gather.6.cloned.1.call-start = ((), (), s32[]{:S(2)}) async-start(), calls=%async_computation.6 | async-start | bytes 2228224 | tf_op jit(solution)/shard_map/all_gather | solution.py:23
  655.5 92.3 %all-reduce.20.cloned.1.call-start = ((), (), s32[]{:S(2)}) async-start(), calls=%async_computation.7 | async-start | bytes 2097152 | tf_op jit(solution)/shard_map/psum | solution.py:26
  729.8 155.4 %all-reduce.22.cloned.1.call-start = ((), (), s32[]{:S(2)}) async-start(), calls=%async_computation.8 | async-start | bytes 4194304 | tf_op jit(solution)/shard_map/psum | solution.py:16
  758.0 260.7 %all-reduce.24.cloned.1.call-start = ((), (), s32[]{:S(2)}) async-start(), calls=%async_computation.9 | async-start | bytes 4194304 | tf_op jit(solution)/shard_map/psum | solution.py:21
  893.2 192.3 %all-gather.8.cloned.1.call-start = ((), (), s32[]{:S(2)}) async-start(), calls=%async_computation.10 | async-start | bytes 2228224 | tf_op jit(solution)/shard_map/all_gather | solution.py:23
  1024.3 92.4 %all-reduce.26.cloned.1.call-start = ((), (), s32[]{:S(2)}) async-start(), calls=%async_computation.11 | async-start | bytes 2097152 | tf_op jit(solution)/shard_map/psum | solution.py:26
  1085.6 13.2 %copy-start.2 = (f32[4096,128]{0,1:T(8,128)S(1)}, f32[4096,128]{0,1:T(8,128)}, u32[]{:S(2)}) copy-start(f32[4096,128]{0,1:T(8,128)} %multiply_add_fusion.1) | copy-start | bytes 6291460
  1101.9 14.8 %copy-start.1 = (f32[2048,128]{0,1:T(8,128)S(1)}, f32[2048,128]{0,1:T(8,128)}, u32[]{:S(2)}) copy-start(f32[2048,128]{0,1:T(8,128)} %all-reduce.14.cloned.1.call-done) | copy-start | bytes 3145732
  1101.9 14.8 %copy-start.3 = (f32[2048,128]{0,1:T(8,128)S(1)}, f32[2048,128]{0,1:T(8,128)}, u32[]{:S(2)}) copy-start(f32[2048,128]{0,1:T(8,128)} %all-reduce.20.cloned.1.call-done) | copy-start | bytes 3145732
Sparse Core Ops, SparseCore 0:
  19.3 128.6 all-reduce.9
  156.2 125.3 all-reduce.11
  287.3 61.0 all-gather.3
  361.6 17.7 all-reduce.13
  389.4 127.1 all-reduce.15
  524.6 125.2 all-reduce.17
  655.7 61.0 all-gather.5
  730.0 17.7 all-reduce.19
  758.1 127.1 all-reduce.21
  893.4 125.3 all-reduce.23
  1024.5 61.0 all-gather.7
  1098.9 17.7 all-reduce.25
where the time goes:
time: 1140 us; the launch traced here: 1130 us
  waiting for transfers between devices  983 us (86%)
  matrix products  112 us (10%)
  between operations  14.5 us (1%)
    psum x3, waiting for transfers between devices, run_group(): grad_total = lax.psum(part_grad, 'row')  377 us
    psum x3, waiting for transfers between devices, run_group(): image = lax.psum(term, 'row')  376 us
    all_gather x3, waiting for transfers between devices, run_group(): update = lax.all_gather(update_own, 'row', axis=0, tiled=True)  183 us
    psum x3, waiting for transfers between devices, run_group(): residual = residual - relaxation * lax.psum(change, 'col')  46.9 us
    dot_general x3, matrix products, run_group(): jnp.dot(samples, update.astype(jnp.bfloat16), preferred_element_type=jnp....  39.2 us
    dot_general x3, matrix products, run_group(): jnp.einsum('rb,rk->bk', samples, res16, preferred_element_type=jnp.float32)  31.9 us
    dot_general x3, matrix products, run_group(): term = jnp.dot(inverse, grad_own, precision=lax.Precision.HIGHEST)  24 us
  transfers between devices with their start and end apart: 12, of which 12 were waited for; matrix products, arithmetic and copies ran while one was open for 1% of the time, Pallas kernels for 0%

commit v1 on v0

--- a/solution.py
+++ b/solution.py
@@ -18,7 +18,7 @@
             lax.dynamic_slice_in_dim(grad_total, offset, own_rows, 0) - ridge_weight * own_solution
         )
         term = jnp.dot(inverse, grad_own, precision=lax.Precision.HIGHEST)
-        image = lax.psum(term, "row")
+        image = jnp.sum(lax.all_gather(term, "row"), axis=0)
         update_own = jnp.einsum("bc,bk->ck", inverse, image, precision=lax.Precision.HIGHEST)
         update = lax.all_gather(update_own, "row", axis=0, tiled=True)
         solution = solution + relaxation * update

time: 1140 us -> 1910 us (1.68)
  waiting for transfers between devices: 983 us -> 1650 us
  local copies, waits for them, and re-layouts: 7.71 us -> 90.5 us
  other arithmetic: 10.3 us -> 39.6 us
    all_gather x0 -> x3, waiting for transfers between devices: none -> 1050 us  [run_group(): image = jnp.sum(lax.all_gather(term, 'row'), axis=0)]
    psum x3 -> x0, waiting for transfers between devices: 376 us -> none  [run_group(): image = lax.psum(term, 'row')]
    unnamed x13 -> x18, local copies, waits for them, and re-layouts: 7.71 us -> 90.5 us
    reduce_sum x0 -> x3, other arithmetic: none -> 26.4 us  [run_group(): image = jnp.sum(lax.all_gather(term, 'row'), axis=0)]
where the time goes in v1:
time: 1910 us
  waiting for transfers between devices  1650 us (86%)
  matrix products  106 us (6%)
  local copies, waits for them, and re-layouts  90.5 us (5%)
  other arithmetic  39.6 us (2%)
    all_gather x3, waiting for transfers between devices, run_group(): image = jnp.sum(lax.all_gather(term, 'row'), axis=0)  1050 us
    psum x3, waiting for transfers between devices, run_group(): grad_total = lax.psum(part_grad, 'row')  376 us
    all_gather x3, waiting for transfers between devices, run_group(): update = lax.all_gather(update_own, 'row', axis=0, tiled=True)  180 us
    unnamed x18, local copies, waits for them, and re-layouts  90.5 us
    psum x3, waiting for transfers between devices, run_group(): residual = residual - relaxation * lax.psum(change, 'col')  46 us
    dot_general x3, matrix products, run_group(): jnp.dot(samples, update.astype(jnp.bfloat16), preferred_element_type=jnp....  39.1 us
  transfers between devices with their start and end apart: 12, of which 12 were waited for; matrix products, arithmetic and copies ran while one was open for 1% of the time, Pallas kernels for 0%

profile of v1, /device:TPU:0, one launch (start us, length us, event | category | flops | bytes accessed | tf_op | source)
XLA Modules:
  0.0 1905.6 jit_solution(1201054184582445515)
XLA Ops:
  7.2 11.9 fusion.23
  19.2 128.8 %all-reduce.7.cloned.1.call-done = f32[4096,128]{1,0:T(8,128)} async-done(((f32[4096,128]{1,0:T(8,128)}), f32[4096,128]{1,0:T(8,128)}) %all-reduce.7.cloned.1.call-update) | async-done | bytes 2097168 | tf_op jit(solution)/shard_map/psum | solution.py:16
  148.0 8.1 convolution_bitcast_fusion.4
  156.3 350.1 %all-gather.16.cloned.1.call-done = f32[65536,128]{0,1:T(8,128)} async-done(((f32[4096,128]{0,1:T(8,128)}), f32[65536,128]{0,1:T(8,128)}) %all-gather.16.cloned.1.call-update) | async-done | bytes 33554448 | tf_op jit(solution)/shard_map/all_gather | solution.py:21
  506.4 28.2 %copy.11 = f32[16,8,16,4096]{3,2,1,0:T(8,128)S(1)} copy(f32[16,8,16,4096]{3,1,2,0:T(8,128)} %bitcast.65) | data formatting | bytes 67108864
  545.4 60.0 %all-gather.10.cloned.1.call-done = f32[4096,128]{0,1:T(8,128)} async-done(((f32[256,128]{0,1:T(8,128)}), f32[4096,128]{0,1:T(8,128)}) %all-gather.10.cloned.1.call-update) | async-done | bytes 2097168 | tf_op jit(solution)/shard_map/all_gather | solution.py:23
  605.5 13.0 convolution_bitcast_fusion.7
  619.3 17.1 all-reduce.9.cloned.1.call-done
  636.5 9.8 convolution_bitcast_fusion.1
  649.4 124.1 %all-reduce.11.cloned.1.call-done = f32[4096,128]{0,1:T(8,128)} async-done(((f32[4096,128]{0,1:T(8,128)}), f32[4096,128]{0,1:T(8,128)}) %all-reduce.11.cloned.1.call-update) | async-done | bytes 2097168 | tf_op jit(solution)/shard_map/psum | solution.py:16
  781.8 350.1 %all-gather.18.cloned.1.call-done = f32[65536,128]{0,1:T(8,128)} async-done(((f32[4096,128]{0,1:T(8,128)}), f32[65536,128]{0,1:T(8,128)}) %all-gather.18.cloned.1.call-update) | async-done | bytes 33554448 | tf_op jit(solution)/shard_map/all_gather | solution.py:21
  1131.9 28.2 %copy.12 = f32[16,8,16,4096]{3,2,1,0:T(8,128)S(1)} copy(f32[16,8,16,4096]{3,1,2,0:T(8,128)} %bitcast.66) | data formatting | bytes 67108864
  1160.2 9.2 bitcast_reduce_fusion.1
  1173.8 60.0 %all-gather.12.cloned.1.call-done = f32[4096,128]{0,1:T(8,128)} async-done(((f32[256,128]{0,1:T(8,128)}), f32[4096,128]{0,1:T(8,128)}) %all-gather.12.cloned.1.call-update) | async-done | bytes 2097168 | tf_op jit(solution)/shard_map/all_gather | solution.py:23
  1233.9 13.0 convolution_bitcast_fusion.6
  1247.2 17.7 all-reduce.13.cloned.1.call-done
  1264.9 9.9 convolution_bitcast_fusion
  1278.7 123.4 %all-reduce.15.cloned.1.call-done = f32[4096,128]{0,1:T(8,128)} async-done(((f32[4096,128]{0,1:T(8,128)}), f32[4096,128]{0,1:T(8,128)}) %all-reduce.15.cloned.1.call-update) | async-done | bytes 2097168 | tf_op jit(solution)/shard_map/psum | solution.py:16
  1410.0 350.3 %all-gather.20.cloned.1.call-done = f32[65536,128]{0,1:T(8,128)} async-done(((f32[4096,128]{0,1:T(8,128)}), f32[65536,128]{0,1:T(8,128)}) %all-gather.20.cloned.1.call-update) | async-done | bytes 33554448 | tf_op jit(solution)/shard_map/all_gather | solution.py:21
  1760.4 28.2 %copy.13 = f32[16,8,16,4096]{3,2,1,0:T(8,128)S(1)} copy(f32[16,8,16,4096]{3,1,2,0:T(8,128)} %bitcast.67) | data formatting | bytes 67108864
  1788.6 9.2 bitcast_reduce_fusion
  1802.3 60.0 %all-gather.14.cloned.1.call-done = f32[4096,128]{0,1:T(8,128)} async-done(((f32[256,128]{0,1:T(8,128)}), f32[4096,128]{0,1:T(8,128)}) %all-gather.14.cloned.1.call-update) | async-done | bytes 2097168 | tf_op jit(solution)/shard_map/all_gather | solution.py:23
  1862.3 13.0 convolution_bitcast_fusion.5
  1882.2 11.1 all-reduce.17.cloned.1.call-done
  (49 shorter events, 56.1 us)
Async XLA Ops:
  7.2 140.8 %all-reduce.7.cloned.1.call-start = ((), (), s32[]{:S(2)}) async-start(), calls=%async_computation | async-start | bytes 4194304 | tf_op jit(solution)/shard_map/psum | solution.py:16
  19.2 487.3 %all-gather.16.cloned.1.call-start = ((), (), s32[]{:S(2)}) async-start(), calls=%async_computation.9 | async-start | bytes 35651584 | tf_op jit(solution)/shard_map/all_gather | solution.py:21
  156.1 449.4 %all-gather.10.cloned.1.call-start = ((), (), s32[]{:S(2)}) async-start(), calls=%async_computation.1 | async-start | bytes 2228224 | tf_op jit(solution)/shard_map/all_gather | solution.py:23
  534.7 7.9 copy-start
  545.4 73.6 %copy-start.5 = (f32[2048,128]{1,0:T(8,128)S(1)}, f32[2048,128]{1,0:T(8,128)}, u32[]{:S(2)}) copy-start(f32[2048,128]{1,0:T(8,128)} %param.4) | copy-start | bytes 3145732
  545.4 91.1 %all-reduce.9.cloned.1.call-start = ((), (), s32[]{:S(2)}) async-start(), calls=%async_computation.2 | async-start | bytes 2097152 | tf_op jit(solution)/shard_map/psum | solution.py:26
  618.5 155.0 %all-reduce.11.cloned.1.call-start = ((), (), s32[]{:S(2)}) async-start(), calls=%async_computation.3 | async-start | bytes 4194304 | tf_op jit(solution)/shard_map/psum | solution.py:16
  646.3 485.7 %all-gather.18.cloned.1.call-start = ((), (), s32[]{:S(2)}) async-start(), calls=%async_computation.10 | async-start | bytes 35651584 | tf_op jit(solution)/shard_map/all_gather | solution.py:21
  781.6 452.3 %all-gather.12.cloned.1.call-start = ((), (), s32[]{:S(2)}) async-start(), calls=%async_computation.4 | async-start | bytes 2228224 | tf_op jit(solution)/shard_map/all_gather | solution.py:23
  1160.2 9.2 copy-start.1
  1173.8 91.1 %copy-start.3 = (f32[2048,128]{0,1:T(8,128)S(1)}, f32[2048,128]{0,1:T(8,128)}, u32[]{:S(2)}) copy-start(f32[2048,128]{0,1:T(8,128)} %all-reduce.9.cloned.1.call-done) | copy-start | bytes 3145732
  1173.8 91.1 %all-reduce.13.cloned.1.call-start = ((), (), s32[]{:S(2)}) async-start(), calls=%async_computation.5 | async-start | bytes 2097152 | tf_op jit(solution)/shard_map/psum | solution.py:26
  1246.9 155.1 %all-reduce.15.cloned.1.call-start = ((), (), s32[]{:S(2)}) async-start(), calls=%async_computation.6 | async-start | bytes 4194304 | tf_op jit(solution)/shard_map/psum | solution.py:16
  1274.8 485.6 %all-gather.20.cloned.1.call-start = ((), (), s32[]{:S(2)}) async-start(), calls=%async_computation.11 | async-start | bytes 35651584 | tf_op jit(solution)/shard_map/all_gather | solution.py:21
  1410.0 452.3 %all-gather.14.cloned.1.call-start = ((), (), s32[]{:S(2)}) async-start(), calls=%async_computation.7 | async-start | bytes 2228224 | tf_op jit(solution)/shard_map/all_gather | solution.py:23
  1788.6 9.3 copy-start.2
  1802.2 91.1 %all-reduce.17.cloned.1.call-start = ((), (), s32[]{:S(2)}) async-start(), calls=%async_computation.8 | async-start | bytes 2097152 | tf_op jit(solution)/shard_map/psum | solution.py:26
  1879.2 14.1 copy-start.4
Sparse Core Ops, SparseCore 0:
  19.3 128.6 all-reduce.6
  156.2 350.2 all-gather.15
  545.5 59.9 all-gather.9
  618.6 17.7 all-reduce.8
  646.4 127.1 all-reduce.10
  781.7 350.2 all-gather.17
  1173.9 59.9 all-gather.11
  1247.0 17.7 all-reduce.12
  1274.9 127.1 all-reduce.14
  1410.1 350.2 all-gather.19
  1802.3 59.9 all-gather.13
  1875.5 17.7 all-reduce.16
